TPU v7x, 512 devices: a whole 4x4x16 slice. The times are simulated.
512 devices in a mesh: ex: 32 (over y, x, core), mp: 16 (over z).
Axes of the slice: x: 4, y: 4, z: 16, core: 2. Of those that a mesh axis runs over, the one named last changes fastest.
Arguments:
- acts: bfloat16 [16, 4096, 4096], P('mp', 'ex'), may hold values from -6 to 6
- grads: bfloat16 [16, 4096, 1024], P('mp', 'ex'), may hold values from -12 to 12
- down_factor: bfloat16 [16, 16, 4096], P('mp'), may hold values from -0.09375 to 0.09375
- up_factor_transposed: bfloat16 [16, 16, 1024], P('mp'), may hold values from -0.1875 to 0.1875
- input_projection: bfloat16 [16, 64, 4096], P('mp'), may hold values from -0.09375 to 0.09375
- gradient_projection: bfloat16 [16, 64, 1024], P('mp'), may hold values from -0.1875 to 0.1875
- order: int32 [16, 32, 16], P('mp', 'ex'), may hold values from 0 to 15, each once within a row
- damping: float32 [1], replicated, may hold values from 0.5 to 2
Outputs:
- features: float32 [512, 1024], P(('ex', 'mp'))
- factor_r: float32 [16, 64, 64], P('mp')
Inputs may be any that keep to these rules, and one draw needn't show every extreme that they name: order[b, m] lists each of the 16 examples of shard m once: stored example e of block b is example order[b, m, e] of that shard.
All inputs are finite; a program needn't handle non-finite values.
Results may differ from a plain program's by a relative error of at most 0.0003.
Values sent between devices are 32-bit elements; how exact they have to be, the bound alone decides.
A program may use at most 64 MiB of HBM per device.

v0:
```python
import math

import jax
import jax.numpy as jnp
from jax import lax
from jax.sharding import PartitionSpec as P

EXAMPLE_LENGTH = 8


def cut_along(shard, dim, length):
    dims = shard.shape
    blocks = shard.reshape(*dims[:dim], length, dims[dim] // length, *dims[dim + 1 :])
    return jnp.moveaxis(blocks, dim, 0)


def summed_on_arrival(shard, axis, dim):
    blocks = cut_along(shard, dim, lax.axis_size(axis))
    arrived = lax.all_to_all(blocks, axis, split_axis=0, concat_axis=0, tiled=True)
    return arrived.sum(axis=0)


def from_everyone(shard, axis):
    length = lax.axis_size(axis)
    return lax.all_to_all(
        jnp.broadcast_to(shard[None], (length, *shard.shape)), axis, 0, 0, tiled=True
    )


def of_everyone(shard, axis):
    return from_everyone(shard, axis).sum(axis=0)


def project_features(rows, weight):
    return lax.dot_general(
        rows, weight, (((1,), (1,)), ((), ())), preferred_element_type=jnp.float32
    )


def channel_gram(rows, adapter_rank, sketch_columns):
    grouped = rows.reshape(rows.shape[0], adapter_rank, sketch_columns)
    return jnp.einsum("eck,ecl->ckl", grouped, grouped, precision=lax.Precision.HIGHEST)


def local(
    acts,
    grads,
    down_factor,
    up_factor_transposed,
    input_projection,
    gradient_projection,
    order,
    damping,
):
    input_rows = acts[0]
    output_gradients = grads[0]
    local_example_rows = input_rows.shape[0] // EXAMPLE_LENGTH
    adapter_rank = down_factor.shape[1]
    sketch_columns = input_projection.shape[1]
    feature_width = adapter_rank * sketch_columns
    scaling = 1.0 / math.sqrt(2.0 * EXAMPLE_LENGTH * lax.axis_size("mp"))
    reduced_gradient = project_features(output_gradients, up_factor_transposed[0]).reshape(
        local_example_rows, EXAMPLE_LENGTH, adapter_rank
    )
    reduced_input = project_features(input_rows, down_factor[0]).reshape(
        local_example_rows, EXAMPLE_LENGTH, adapter_rank
    )
    sketch_in = project_features(input_rows, input_projection[0]).reshape(
        local_example_rows, EXAMPLE_LENGTH, sketch_columns
    )
    sketch_out = project_features(output_gradients, gradient_projection[0]).reshape(
        local_example_rows, EXAMPLE_LENGTH, sketch_columns
    )
    first = jnp.einsum("etc,etk->eck", reduced_gradient, sketch_in, precision=lax.Precision.HIGHEST)
    second = jnp.einsum("etc,etk->eck", reduced_input, sketch_out, precision=lax.Precision.HIGHEST)
    partial_value = (first + second).reshape(local_example_rows, feature_width) * scaling
    stored = order[0, 0]
    per_device = local_example_rows // lax.axis_size("mp")
    row_ids = jnp.arange(per_device * lax.axis_size("mp"), dtype=jnp.int32)
    selector = (row_ids[:, None] == stored[None, :]).astype(jnp.float32)
    own_rows = summed_on_arrival(
        jnp.dot(selector, partial_value, precision=lax.Precision.HIGHEST), "mp", 0
    )
    all_examples = local_example_rows * lax.axis_size("ex")
    part_channels = adapter_rank // lax.axis_size("mp")
    channel_rows = lax.all_to_all(own_rows, "mp", split_axis=1, concat_axis=0, tiled=True)
    local_gram = channel_gram(channel_rows, part_channels, sketch_columns)
    own_blocks = of_everyone(local_gram, "ex")
    system = (
        own_blocks / all_examples
        + damping[0] * jnp.eye(sketch_columns, dtype=jnp.float32)[None, :, :]
    )
    r_block = jnp.swapaxes(jnp.linalg.cholesky(system), 1, 2)
    return (own_rows, r_block)


def solution(mesh):
    in_specs = (
        P("mp", "ex", None),
        P("mp", "ex", None),
        P("mp", None, None),
        P("mp", None, None),
        P("mp", None, None),
        P("mp", None, None),
        P("mp", "ex", None),
        P(),
    )
    out_specs = (P(("ex", "mp"), None), P("mp", None, None))
    return jax.shard_map(local, mesh=mesh, in_specs=in_specs, out_specs=out_specs, check_vma=False)
```

profile of v0, /device:TPU:1, one launch (start us, length us, event | category | flops | bytes accessed | tf_op | source)
XLA Modules:
  0.0 84.0 jit_solution(253056376458362535)
XLA Ops:
  0.7 1.2 %copy-done = bf16[1,128,4096]{2,1,0:T(8,128)(2,1)S(1)} copy-done((bf16[1,128,4096]{2,1,0:T(8,128)(2,1)S(1)}, bf16[1,128,4096]{2,1,0:T(8,128)(2,1)}, u32[]{:S(2)}) %copy-start) | copy-done | bytes 1048600
  1.9 1.5 %fusion.3 = f32[16,8,64]{2,1,0:T(8,128)S(1)} fusion(bf16[1,128,4096]{2,1,0:T(8,128)(2,1)S(1)} %copy-done, bf16[1,64,4096]{2,1,0:T(8,128)(2,1)} %param.12), kind=kOutput, calls=%fused_computation.5 | convolution fusion | flops 67108864 | bytes 1605632 | tf_op jit(solution)/shard_map/dot_general | solution.py:35
  3.4 0.4 fusion.1
  3.8 0.5 copy-done.1
  4.3 0.2 fusion.8
  4.5 0.7 copy-done.3
  5.2 0.2 fusion.6
  5.4 0.4 fusion.15
  5.9 0.4 fusion
  6.4 0.6 copy-done.6
  7.0 0.2 convolution_bitcast_fusion
  7.3 27.1 %all_to_all.23 = f32[16,1,1024]{2,1,0:T(1,128)S(1)} all-to-all(f32[16,1,1024]{2,1,0:T(1,128)S(1)} %copy.17), channel_id=1, replica_groups=mesh['ex'=32,'mp'=16] {'mp'}, dimensions={0} | all-to-all | bytes 131072 | tf_op jit(solution)/shard_map/all_to_all | solution.py:19
  34.5 0.5 copy-done.5
  35.0 14.3 %all_to_all.24 = f32[1,16,64]{2,0,1:T(1,128)S(1)} all-to-all(f32[1,16,64]{2,0,1:T(1,128)S(1)} %all_to_all.17), channel_id=1, replica_groups=mesh['ex'=32,'mp'=16] {'mp'}, dimensions={1} | all-to-all | bytes 8192 | tf_op jit(solution)/shard_map/all_to_all | solution.py:86
  49.3 0.2 fusion.16
  49.7 1.4 %reshape.109 = f32[32,1,4096]{2,1,0:T(1,128)} reshape(f32[32,1,64,64]{3,2,1,0:T(8,128)S(1)} %broadcast_in_dim.4) | data formatting | bytes 1048576
  51.1 10.2 %all-to-all-start.2 = ((f32[32,1,4096]{2,1,0:T(1,128)}), f32[32,1,4096]{2,1,0:T(1,128)S(1)}, u32[]{:S(2)}, u32[]{:S(2)}) async-start(f32[32,1,4096]{2,1,0:T(1,128)} %reshape.109), calls=%async_computation.2 | async-start | bytes 1048576 | tf_op jit(solution)/shard_map/all_to_all | solution.py:25
  62.0 10.8 %all-to-all-done.2 = f32[32,1,4096]{2,1,0:T(1,128)S(1)} async-done(((f32[32,1,4096]{2,1,0:T(1,128)}), f32[32,1,4096]{2,1,0:T(1,128)S(1)}, u32[]{:S(2)}, u32[]{:S(2)}) %all-to-all-start.2) | async-done | bytes 524320 | tf_op jit(solution)/shard_map/all_to_all | solution.py:25
  72.8 0.5 broadcast.74
  73.3 1.9 %reduce.11 = f32[32,4096]{1,0:T(8,128)S(1)} reduce(f32[32,1,4096]{2,1,0:T(1,128)S(1)} %all-to-all-done.2, f32[]{:T(128)} %broadcast.74), dimensions={1}, to_apply=%all_to_all.19.reduce_sub_computation | reduce | bytes 1048580 | tf_op jit(solution)/shard_map/all_to_all | solution.py:25
  75.2 0.4 reshape.110
  75.9 5.8 %custom-call.4 = f32[1,64,64]{2,1,0:T(8,128)S(1)} custom-call(f32[1,64,64]{2,1,0:T(8,128)S(1)} %fusion.12), custom_call_target="Cholesky" | custom-call | tf_op jit(solution)/shard_map/jit(cholesky)/cholesky | solution.py:93
  81.9 0.7 compare_reduce_fusion
  82.7 1.3 %select_bitcast_fusion = f32[1,64,64]{2,1,0:T(8,128)} fusion(f32[1,64,64]{1,2,0:T(8,128)S(1)} %copy.20, pred[]{:T(512)} %compare_reduce_fusion), kind=kLoop, calls=%fused_computation.18 | loop fusion | flops 12288 | bytes 32769 | tf_op jit(solution)/shard_map/transpose | solution.py:93
  (21 shorter events, 0.9 us)
Async XLA Ops:
  0.6 1.2 %copy-start = (bf16[1,128,4096]{2,1,0:T(8,128)(2,1)S(1)}, bf16[1,128,4096]{2,1,0:T(8,128)(2,1)}, u32[]{:S(2)}) copy-start(bf16[1,128,4096]{2,1,0:T(8,128)(2,1)} %param.8) | copy-start | bytes 3145732
  0.6 2.7 %copy-start.2 = (bf16[1,16,4096]{2,1,0:T(8,128)(2,1)S(1)}, bf16[1,16,4096]{2,1,0:T(8,128)(2,1)}, u32[]{:S(2)}) copy-start(bf16[1,16,4096]{2,1,0:T(8,128)(2,1)} %param.10) | copy-start | bytes 393220
  3.3 1.0 %copy-start.1 = (bf16[1,128,1024]{2,1,0:T(8,128)(2,1)S(1)}, bf16[1,128,1024]{2,1,0:T(8,128)(2,1)}, u32[]{:S(2)}) copy-start(bf16[1,128,1024]{2,1,0:T(8,128)(2,1)} %param.9) | copy-start | bytes 786436
  3.4 0.9 %copy-start.4 = (bf16[1,16,1024]{2,1,0:T(8,128)(2,1)S(1)}, bf16[1,16,1024]{2,1,0:T(8,128)(2,1)}, u32[]{:S(2)}) copy-start(bf16[1,16,1024]{2,1,0:T(8,128)(2,1)} %param.11) | copy-start | bytes 98308
  4.3 0.9 %copy-start.3 = (bf16[1,64,1024]{2,1,0:T(8,128)(2,1)S(1)}, bf16[1,64,1024]{2,1,0:T(8,128)(2,1)}, u32[]{:S(2)}) copy-start(bf16[1,64,1024]{2,1,0:T(8,128)(2,1)} %param.13) | copy-start | bytes 393220
  6.4 0.7 copy-start.6
  34.4 0.6 copy-start.5
  51.1 21.6 %all-to-all-start.2 = ((f32[32,1,4096]{2,1,0:T(1,128)}), f32[32,1,4096]{2,1,0:T(1,128)S(1)}, u32[]{:S(2)}, u32[]{:S(2)}) async-start(f32[32,1,4096]{2,1,0:T(1,128)} %reshape.109), calls=%async_computation.2 | async-start | bytes 1048576 | tf_op jit(solution)/shard_map/all_to_all | solution.py:25
where the time goes:
time: 84.4 us; the launch traced here: 84 us
  blocking collectives  41.4 us (49%)
  waiting for transfers between devices  10.8 us (13%)
  starting transfers between devices  10.2 us (12%)
  other arithmetic  10.1 us (12%)
  local copies, waits for them, and re-layouts  6.54 us (8%)
  matrix products  3.54 us (4%)
  between operations  1.46 us (2%)
    all_to_all x1, blocking collectives, summed_on_arrival(): lax.all_to_all(blocks, axis, split_axis=0, concat_axis=0, tiled=True)  27.1 us
    all_to_all x1, blocking collectives, local(): lax.all_to_all(own_rows, 'mp', split_axis=1, concat_axis=0, tiled=True)  14.3 us
    all_to_all x1, waiting for transfers between devices, from_everyone(): lax.all_to_all(jnp.broadcast_to(shard[None], (length, *shard.shape)), axi...  10.8 us
    all_to_all x1, starting transfers between devices, from_everyone(): lax.all_to_all(jnp.broadcast_to(shard[None], (length, *shard.shape)), axi...  10.2 us
    another operation x3, other arithmetic, local(): r_block = jnp.swapaxes(jnp.linalg.cholesky(system), 1, 2)  6.69 us
    unnamed x16, local copies, waits for them, and re-layouts  5.45 us
    dot_general x4, matrix products, project_features(): lax.dot_general(rows, weight, (((1,), (1,)), ((), ())), preferred_element...  2.3 us
    all_to_all x1, other arithmetic, from_everyone(): lax.all_to_all(jnp.broadcast_to(shard[None], (length, *shard.shape)), axi...  1.89 us
  transfers between devices with their start and end apart: 1, of which 1 were waited for; matrix products, arithmetic and copies ran while one was open for 0% of the time, Pallas kernels for 0%

commit v1 on v0

v1 whole, which is shorter than its diff:
```python
import functools
import math

import jax
import jax.numpy as jnp
from jax import lax
from jax.experimental import pallas as pl
from jax.experimental.pallas import tpu as pltpu
from jax.sharding import PartitionSpec as P

EXAMPLE_LENGTH = 8
CHUNKS = 4
MESH = pl.DeviceIdType.MESH


def nt(a, b):
    return lax.dot_general(a, b, (((1,), (1,)), ((), ())), preferred_element_type=jnp.float32)


def halves(x):
    high = x.astype(jnp.bfloat16)
    return high, (x - high.astype(jnp.float32)).astype(jnp.bfloat16)


def outward(step, n):
    turn = lax.rem(step + 1, 2)
    return n // 2 + ((step + 1) // 2) * (1 - 2 * turn)


def wait_bytes(buf, count, sem):
    part = buf.at[pl.ds(0, count)]
    pltpu.make_async_copy(part, part, sem).wait()


def factor(blocks, r_ref, size):
    lane = lax.broadcasted_iota(jnp.int32, (1, size), 1)
    blocks = list(blocks)
    for k in range(size):
        at, sub = k // 8, k % 8
        row = blocks[at][sub : sub + 1, :]
        pivot = row[:, k : k + 1]
        r_ref[0, k : k + 1, :] = jnp.where(lane >= k, row * lax.rsqrt(pivot), 0.0)
        if k + 1 < size:
            scaled = row * (1.0 / pivot)
            for b in range((k + 1) // 8, size // 8):
                blocks[b] = blocks[b] - blocks[b][:, k : k + 1] * scaled


def kernel(
    n_ex,
    n_mp,
    scaling,
    acts,
    grads,
    down,
    up,
    in_proj,
    g_proj,
    order,
    damping,
    out_f,
    out_r,
    a_v,
    g_v,
    wa_v,
    wg_v,
    zsend,
    zrecv,
    fbuf,
    xbuf,
    rowsend,
    rowrecv,
    load_sem,
    send_sem,
    recv_sem,
):
    ex = lax.axis_index("ex")
    mp = lax.axis_index("mp")
    rank = down.shape[1]
    sketch = in_proj.shape[1]
    width = a_v.shape[1] // CHUNKS

    g_copies = [
        pltpu.make_async_copy(up.at[0], wg_v.at[pl.ds(0, rank)], load_sem.at[0]),
        pltpu.make_async_copy(g_proj.at[0], wg_v.at[pl.ds(rank, sketch)], load_sem.at[1]),
        pltpu.make_async_copy(grads.at[0], g_v, load_sem.at[2]),
    ]
    a_copies = []
    for i in range(CHUNKS):
        cols = pl.ds(i * width, width)
        a_copies.append(
            [
                pltpu.make_async_copy(
                    down.at[0, :, cols], wa_v.at[pl.ds(0, rank), cols], load_sem.at[3 + 3 * i]
                ),
                pltpu.make_async_copy(
                    in_proj.at[0, :, cols], wa_v.at[pl.ds(rank, sketch), cols], load_sem.at[4 + 3 * i]
                ),
                pltpu.make_async_copy(acts.at[0, :, cols], a_v.at[:, cols], load_sem.at[5 + 3 * i]),
            ]
        )
    for copy in g_copies:
        copy.start()
    for chunk in a_copies:
        for copy in chunk:
            copy.start()

    barrier = pltpu.get_barrier_semaphore()

    def greet(axis, n, me):
        def body(s, _):
            dst = lax.rem(me + outward(s, n), n)
            pl.semaphore_signal(barrier, inc=1, device_id={axis: dst}, device_id_type=MESH)
            return 0

        lax.fori_loop(0, n - 1, body, 0)

    greet("mp", n_mp, mp)
    greet("ex", n_ex, ex)

    tokens = a_v.shape[0]
    spread = (
        lax.broadcasted_iota(jnp.int32, (rank, tokens), 1) // EXAMPLE_LENGTH
        == lax.broadcasted_iota(jnp.int32, (rank, tokens), 0)
    ).astype(jnp.float32)
    stored = jnp.broadcast_to(order[0].astype(jnp.float32), (16, 16)).astype(jnp.bfloat16)
    target = lax.dot_general(
        stored,
        spread.astype(jnp.bfloat16),
        (((1,), (0,)), ((), ())),
        preferred_element_type=jnp.float32,
    )
    rows = lax.broadcasted_iota(jnp.int32, (16, tokens), 0).astype(jnp.float32)
    place = jnp.where(target == rows, scaling, 0.0)

    for copy in g_copies:
        copy.wait()
    from_g = nt(wg_v[...], g_v[...])
    from_a = jnp.zeros((rank + sketch, tokens), jnp.float32)
    for i in range(CHUNKS):
        for copy in a_copies[i]:
            copy.wait()
        cols = slice(i * width, (i + 1) * width)
        from_a = from_a + nt(wa_v[:, cols], a_v[:, cols])

    low = [from_g[:rank], from_a[:rank]]
    left = jnp.concatenate(
        [
            jnp.concatenate(
                [
                    (x[:, None, :] * place[None, h * 8 : h * 8 + 8]).reshape(rank * 8, tokens)
                    for x in low
                ],
                axis=1,
            )
            for h in range(2)
        ],
        axis=0,
    )
    right = jnp.concatenate([from_a[rank:], from_g[rank:]], axis=1)
    left_h, left_l = halves(left)
    right_h, right_l = halves(right)
    part = nt(left_h, right_h) + (nt(left_h, right_l) + nt(left_l, right_h))
    tiles = jnp.concatenate([part[: rank * 8], part[rank * 8 :]], axis=1)
    zsend[...] = tiles.reshape(rank, 8, 2 * sketch)

    pl.semaphore_wait(barrier, n_mp + n_ex - 2)

    def send_z(s, _):
        dst = lax.rem(mp + outward(s, n_mp), n_mp)
        pltpu.make_async_remote_copy(
            src_ref=zsend.at[dst],
            dst_ref=zrecv.at[mp],
            send_sem=send_sem.at[0],
            recv_sem=recv_sem.at[0],
            device_id={"mp": dst},
            device_id_type=MESH,
        ).start()
        return 0

    lax.fori_loop(0, n_mp - 1, send_z, 0)
    zrecv[mp] = zsend[mp]
    wait_bytes(zrecv, n_mp - 1, recv_sem.at[0])
    mine = jnp.sum(zrecv[...], axis=0)
    fbuf[...] = mine
    xbuf[ex] = mine

    def send_x(s, _):
        dst = lax.rem(ex + outward(s, n_ex), n_ex)
        pltpu.make_async_remote_copy(
            src_ref=fbuf,
            dst_ref=xbuf.at[ex],
            send_sem=send_sem.at[1],
            recv_sem=recv_sem.at[1],
            device_id={"ex": dst},
            device_id_type=MESH,
        ).start()
        return 0

    lax.fori_loop(0, n_ex - 1, send_x, 0)

    lane = lax.broadcasted_iota(jnp.int32, (8, 2 * sketch), 1)
    turned = jnp.concatenate([mine[:, sketch:], mine[:, :sketch]], axis=1)
    lower = jnp.where(lane < sketch, mine, turned)
    upper = jnp.where(lane < sketch, turned, mine)
    for r in range(8):
        rowsend[r] = lower[r : r + 1]
        rowsend[r + 8] = upper[r : r + 1]

    def send_rows(s, _):
        dst = lax.rem(mp + outward(s, n_mp), n_mp)
        pltpu.make_async_remote_copy(
            src_ref=rowsend.at[dst],
            dst_ref=rowrecv.at[mp],
            send_sem=send_sem.at[2],
            recv_sem=recv_sem.at[2],
            device_id={"mp": dst},
            device_id_type=MESH,
        ).start()
        return 0

    lax.fori_loop(0, n_mp - 1, send_rows, 0)
    rowrecv[mp] = rowsend[mp]

    wait_bytes(xbuf, n_ex - 1, recv_sem.at[1])
    every = xbuf[...].reshape(n_ex * 8, 2 * sketch)
    square = lax.dot_general(
        every,
        every,
        (((0,), (0,)), ((), ())),
        preferred_element_type=jnp.float32,
        precision=lax.Precision.HIGHEST,
    )
    gram = square[:sketch, :sketch] + square[sketch:, sketch:]
    diag = lax.broadcasted_iota(jnp.int32, (sketch, sketch), 0) == lax.broadcasted_iota(
        jnp.int32, (sketch, sketch), 1
    )
    system = gram * (1.0 / (n_ex * 16)) + jnp.where(diag, damping[0], 0.0)
    factor([system[b * 8 : b * 8 + 8] for b in range(sketch // 8)], out_r, sketch)

    wait_bytes(rowrecv, n_mp - 1, recv_sem.at[2])
    low_lane = lax.broadcasted_iota(jnp.int32, (1, 2 * sketch), 1) < sketch
    for p in range(rank // 2):
        out_f[:, p * 2 * sketch : (p + 1) * 2 * sketch] = jnp.where(
            low_lane, rowrecv[2 * p], rowrecv[2 * p + 1]
        )
    wait_bytes(zsend, n_mp - 1, send_sem.at[0])
    wait_bytes(xbuf, n_ex - 1, send_sem.at[1])
    wait_bytes(rowsend, n_mp - 1, send_sem.at[2])


def local(n_ex, n_mp, *args):
    acts, grads, down, up, in_proj, g_proj, order, damping = args
    rank, sketch = down.shape[1], in_proj.shape[1]
    scaling = 1.0 / math.sqrt(2.0 * EXAMPLE_LENGTH * n_mp)
    f32 = jnp.float32
    return pl.pallas_call(
        functools.partial(kernel, n_ex, n_mp, scaling),
        out_shape=(
            jax.ShapeDtypeStruct((1, rank * sketch), f32),
            jax.ShapeDtypeStruct((1, sketch, sketch), f32),
        ),
        in_specs=[pl.BlockSpec(memory_space=pl.ANY)] * 6
        + [
            pl.BlockSpec(memory_space=pltpu.VMEM),
            pl.BlockSpec(memory_space=pltpu.SMEM),
        ],
        out_specs=(
            pl.BlockSpec(memory_space=pltpu.VMEM),
            pl.BlockSpec(memory_space=pltpu.VMEM),
        ),
        scratch_shapes=[
            pltpu.VMEM(acts.shape[1:], acts.dtype),
            pltpu.VMEM(grads.shape[1:], grads.dtype),
            pltpu.VMEM((rank + sketch, acts.shape[2]), acts.dtype),
            pltpu.VMEM((rank + sketch, grads.shape[2]), grads.dtype),
            pltpu.VMEM((n_mp, 8, 2 * sketch), f32),
            pltpu.VMEM((n_mp, 8, 2 * sketch), f32),
            pltpu.VMEM((8, 2 * sketch), f32),
            pltpu.VMEM((n_ex, 8, 2 * sketch), f32),
            pltpu.VMEM((n_mp, 1, 2 * sketch), f32),
            pltpu.VMEM((n_mp, 1, 2 * sketch), f32),
            pltpu.SemaphoreType.DMA((3 + 3 * CHUNKS,)),
            pltpu.SemaphoreType.DMA((3,)),
            pltpu.SemaphoreType.DMA((3,)),
        ],
        compiler_params=pltpu.CompilerParams(collective_id=0, has_side_effects=True),
        name="trak",
    )(acts, grads, down, up, in_proj, g_proj, order, damping)


def solution(mesh):
    in_specs = (
        P("mp", "ex", None),
        P("mp", "ex", None),
        P("mp", None, None),
        P("mp", None, None),
        P("mp", None, None),
        P("mp", None, None),
        P("mp", "ex", None),
        P(),
    )
    out_specs = (P(("ex", "mp"), None), P("mp", None, None))
    body = functools.partial(local, mesh.shape["ex"], mesh.shape["mp"])
    return jax.shard_map(body, mesh=mesh, in_specs=in_specs, out_specs=out_specs, check_vma=False)
```

time: 84.4 us -> 40.9 us (0.48)
  blocking collectives: 41.4 us -> 0 us
  Pallas kernels: 0 us -> 36.7 us
  waiting for transfers between devices: 10.8 us -> 0 us
  starting transfers between devices: 10.2 us -> 0 us
  other arithmetic: 10.1 us -> 0 us
  local copies, waits for them, and re-layouts: 6.54 us -> 2.65 us
  matrix products: 3.54 us -> 0 us
    all_to_all x2 -> x0, blocking collectives: 41.4 us -> none  [the longest x1 27.1 us: summed_on_arrival(): lax.all_to_all(blocks, axis, split_axis=0, concat_axis=0, tiled=True)]
    pallas_call x0 -> x1, Pallas kernels: none -> 36.7 us  [local(): pl.pallas_call(functools.partial(kernel, n_ex, n_mp, scaling), out_shape=...]
    all_to_all x1 -> x0, waiting for transfers between devices: 10.8 us -> none  [from_everyone(): lax.all_to_all(jnp.broadcast_to(shard[None], (length, *shard.shape)), axi...]
    all_to_all x1 -> x0, starting transfers between devices: 10.2 us -> none  [from_everyone(): lax.all_to_all(jnp.broadcast_to(shard[None], (length, *shard.shape)), axi...]
    another operation x3 -> x0, other arithmetic: 6.69 us -> none  [local(): r_block = jnp.swapaxes(jnp.linalg.cholesky(system), 1, 2)]
    dot_general x8 -> x0, matrix products: 3.54 us -> none  [the longest x4 2.3 us: project_features(): lax.dot_general(rows, weight, (((1,), (1,)), ((), ())), preferred_element...]
    unnamed x16 -> x2, local copies, waits for them, and re-layouts: 5.45 us -> 2.65 us
    all_to_all x1 -> x0, other arithmetic: 1.89 us -> none  [from_everyone(): lax.all_to_all(jnp.broadcast_to(shard[None], (length, *shard.shape)), axi...]
  transfers between devices with their start and end apart: 1 -> 0, of which waited for: 1 -> 0; matrix products, arithmetic and copies ran while one was open for 0% -> 0% of each run, Pallas kernels for 0% -> 0%
where the time goes in v1:
time: 40.9 us; the launch traced here: 40.7 us
  Pallas kernels  36.7 us (90%)
  local copies, waits for them, and re-layouts  2.65 us (6%)
  between operations  1.29 us (3%)
    pallas_call x1, Pallas kernels, local(): pl.pallas_call(functools.partial(kernel, n_ex, n_mp, scaling), out_shape=...  36.7 us
    unnamed x2, local copies, waits for them, and re-layouts  2.65 us

profile of v1, /device:TPU:1, one launch (start us, length us, event | category | flops | bytes accessed | tf_op | source)
XLA Modules:
  0.0 40.7 jit_solution(4014921137467695056)
XLA Ops:
  1.3 36.7 %trak.1 = (f32[1,1024]{1,0:T(1,128)}, f32[1,64,64]{2,1,0:T(8,128)}) custom-call(bf16[1,128,4096]{2,1,0:T(8,128)(2,1)} %acts.1, bf16[1,128,1024]{2,1,0:T(8,128)(2,1)} %grads.1, bf16[1,16,4096]{2,1,0:T(8,128)(2,1)} %down.1, bf16[1,16,1024]{2,1,0:T(8,128)(2,1)} %up.1, bf16[1,64,4096]{2,1,0:T(8,128)(2,1)} %in_proj.1, bf16[1,64,1024]{2,1,0:T(8,128)(2,1)} %g_proj.1, ...), custom_call_target="tpu_custom_call" | custom-call | tf_op jit(solution)/shard_map/trak/pallas_call | solution.py:257
  38.0 1.3 %copy.13 = f32[1,1024]{1,0:T(1,128)} copy(f32[1,1024]{1,0:T(1,128)} %get-tuple-element.4) | data formatting | bytes 8192
  39.3 1.4 %copy.14 = f32[1,64,64]{2,1,0:T(8,128)} copy(f32[1,64,64]{2,1,0:T(8,128)} %get-tuple-element.5) | data formatting | bytes 32768

commit v2 on v1

--- a/solution.py
+++ b/solution.py
@@ -33,17 +33,55 @@
 
 
 def factor(blocks, r_ref, size):
-    lane = lax.broadcasted_iota(jnp.int32, (1, size), 1)
+    lane = lax.broadcasted_iota(jnp.int32, (8, size), 1)
+    subl = lax.broadcasted_iota(jnp.int32, (8, size), 0)
     blocks = list(blocks)
-    for k in range(size):
-        at, sub = k // 8, k % 8
-        row = blocks[at][sub : sub + 1, :]
-        pivot = row[:, k : k + 1]
-        r_ref[0, k : k + 1, :] = jnp.where(lane >= k, row * lax.rsqrt(pivot), 0.0)
-        if k + 1 < size:
-            scaled = row * (1.0 / pivot)
-            for b in range((k + 1) // 8, size // 8):
-                blocks[b] = blocks[b] - blocks[b][:, k : k + 1] * scaled
+    count = size // 8
+    for q in range(count):
+        k0 = q * 8
+        top = blocks[q]
+        cols = {
+            b: [jnp.broadcast_to(blocks[b][:, k0 + j : k0 + j + 1], (8, size)) for j in range(8)]
+            for b in range(q, count)
+        }
+        pivots = []
+        rows = []
+        scaled = []
+        for j in range(8):
+            pivot = jnp.broadcast_to(cols[q][j][j : j + 1, :], (8, size))
+            inverse = 1.0 / pivot
+            pivots.append(pivot)
+            row = jnp.broadcast_to(top[j : j + 1, :], (8, size))
+            step = row * inverse
+            rows.append(row)
+            scaled.append(step)
+            top = top - cols[q][j] * step
+            for i in range(j + 1, 8):
+                ratio = jnp.broadcast_to(cols[q][i][j : j + 1, :], (8, size)) * inverse
+                for b in range(q, count):
+                    cols[b][i] = cols[b][i] - cols[b][j] * ratio
+        whole, scale = rows[7], pivots[7]
+        for j in range(7):
+            whole = jnp.where(subl == j, rows[j], whole)
+            scale = jnp.where(subl == j, pivots[j], scale)
+        r_ref[0, k0 : k0 + 8, :] = jnp.where(lane >= subl + k0, whole * lax.rsqrt(scale), 0.0)
+        for b in range(q + 1, count):
+            for j in range(8):
+                blocks[b] = blocks[b] - cols[b][j] * scaled[j]
+
+
+def finish(gram, rowrecv, damping, out_f, out_r):
+    size = gram.shape[0]
+    diag = lax.broadcasted_iota(jnp.int32, (size, size), 0) == lax.broadcasted_iota(
+        jnp.int32, (size, size), 1
+    )
+    full = gram[...] + jnp.where(diag, damping[0], 0.0)
+    factor([full[b * 8 : b * 8 + 8] for b in range(size // 8)], out_r, size)
+    low_lane = lax.broadcasted_iota(jnp.int32, (1, 2 * size), 1) < size
+    for p in range(rowrecv.shape[0] // 2):
+        out_f[:, p * 2 * size : (p + 1) * 2 * size] = jnp.where(
+            low_lane, rowrecv[2 * p], rowrecv[2 * p + 1]
+        )
 
 
 def kernel(
@@ -57,9 +95,8 @@
     in_proj,
     g_proj,
     order,
-    damping,
-    out_f,
-    out_r,
+    out_s,
+    rowrecv,
     a_v,
     g_v,
     wa_v,
@@ -69,7 +106,7 @@
     fbuf,
     xbuf,
     rowsend,
-    rowrecv,
+    order_v,
     load_sem,
     send_sem,
     recv_sem,
@@ -99,23 +136,25 @@
                 pltpu.make_async_copy(acts.at[0, :, cols], a_v.at[:, cols], load_sem.at[5 + 3 * i]),
             ]
         )
+    order_copy = pltpu.make_async_copy(order, order_v, load_sem.at[3 + 3 * CHUNKS])
+
+    barrier = pltpu.get_barrier_semaphore()
+
+    def greet(axis, n, me):
+        def body(s, _):
+            dst = lax.rem(me + outward(s, n), n)
+            pl.semaphore_signal(barrier, inc=1, device_id={axis: dst}, device_id_type=MESH)
+            return 0
+
+        lax.fori_loop(0, n - 1, body, 0)
+
+    greet("mp", n_mp, mp)
+    order_copy.start()
     for copy in g_copies:
         copy.start()
     for chunk in a_copies:
         for copy in chunk:
             copy.start()
-
-    barrier = pltpu.get_barrier_semaphore()
-
-    def greet(axis, n, me):
-        def body(s, _):
-            dst = lax.rem(me + outward(s, n), n)
-            pl.semaphore_signal(barrier, inc=1, device_id={axis: dst}, device_id_type=MESH)
-            return 0
-
-        lax.fori_loop(0, n - 1, body, 0)
-
-    greet("mp", n_mp, mp)
     greet("ex", n_ex, ex)
 
     tokens = a_v.shape[0]
@@ -123,7 +162,8 @@
         lax.broadcasted_iota(jnp.int32, (rank, tokens), 1) // EXAMPLE_LENGTH
         == lax.broadcasted_iota(jnp.int32, (rank, tokens), 0)
     ).astype(jnp.float32)
-    stored = jnp.broadcast_to(order[0].astype(jnp.float32), (16, 16)).astype(jnp.bfloat16)
+    order_copy.wait()
+    stored = jnp.broadcast_to(order_v[0].astype(jnp.float32), (16, 16)).astype(jnp.bfloat16)
     target = lax.dot_general(
         stored,
         spread.astype(jnp.bfloat16),
@@ -231,19 +271,8 @@
         preferred_element_type=jnp.float32,
         precision=lax.Precision.HIGHEST,
     )
-    gram = square[:sketch, :sketch] + square[sketch:, sketch:]
-    diag = lax.broadcasted_iota(jnp.int32, (sketch, sketch), 0) == lax.broadcasted_iota(
-        jnp.int32, (sketch, sketch), 1
-    )
-    system = gram * (1.0 / (n_ex * 16)) + jnp.where(diag, damping[0], 0.0)
-    factor([system[b * 8 : b * 8 + 8] for b in range(sketch // 8)], out_r, sketch)
-
+    out_s[...] = (square[:sketch, :sketch] + square[sketch:, sketch:]) * (1.0 / (n_ex * 16))
     wait_bytes(rowrecv, n_mp - 1, recv_sem.at[2])
-    low_lane = lax.broadcasted_iota(jnp.int32, (1, 2 * sketch), 1) < sketch
-    for p in range(rank // 2):
-        out_f[:, p * 2 * sketch : (p + 1) * 2 * sketch] = jnp.where(
-            low_lane, rowrecv[2 * p], rowrecv[2 * p + 1]
-        )
     wait_bytes(zsend, n_mp - 1, send_sem.at[0])
     wait_bytes(xbuf, n_ex - 1, send_sem.at[1])
     wait_bytes(rowsend, n_mp - 1, send_sem.at[2])
@@ -254,21 +283,15 @@
     rank, sketch = down.shape[1], in_proj.shape[1]
     scaling = 1.0 / math.sqrt(2.0 * EXAMPLE_LENGTH * n_mp)
     f32 = jnp.float32
-    return pl.pallas_call(
+    vmem = pl.BlockSpec(memory_space=pltpu.VMEM)
+    gram, row_parts = pl.pallas_call(
         functools.partial(kernel, n_ex, n_mp, scaling),
         out_shape=(
-            jax.ShapeDtypeStruct((1, rank * sketch), f32),
-            jax.ShapeDtypeStruct((1, sketch, sketch), f32),
+            jax.ShapeDtypeStruct((sketch, sketch), f32),
+            jax.ShapeDtypeStruct((n_mp, 1, 2 * sketch), f32),
         ),
-        in_specs=[pl.BlockSpec(memory_space=pl.ANY)] * 6
-        + [
-            pl.BlockSpec(memory_space=pltpu.VMEM),
-            pl.BlockSpec(memory_space=pltpu.SMEM),
-        ],
-        out_specs=(
-            pl.BlockSpec(memory_space=pltpu.VMEM),
-            pl.BlockSpec(memory_space=pltpu.VMEM),
-        ),
+        in_specs=[pl.BlockSpec(memory_space=pl.ANY)] * 7,
+        out_specs=(vmem, vmem),
         scratch_shapes=[
             pltpu.VMEM(acts.shape[1:], acts.dtype),
             pltpu.VMEM(grads.shape[1:], grads.dtype),
@@ -279,14 +302,24 @@
             pltpu.VMEM((8, 2 * sketch), f32),
             pltpu.VMEM((n_ex, 8, 2 * sketch), f32),
             pltpu.VMEM((n_mp, 1, 2 * sketch), f32),
-            pltpu.VMEM((n_mp, 1, 2 * sketch), f32),
-            pltpu.SemaphoreType.DMA((3 + 3 * CHUNKS,)),
+            pltpu.VMEM(order.shape, order.dtype),
+            pltpu.SemaphoreType.DMA((4 + 3 * CHUNKS,)),
             pltpu.SemaphoreType.DMA((3,)),
             pltpu.SemaphoreType.DMA((3,)),
         ],
         compiler_params=pltpu.CompilerParams(collective_id=0, has_side_effects=True),
         name="trak",
-    )(acts, grads, down, up, in_proj, g_proj, order, damping)
+    )(acts, grads, down, up, in_proj, g_proj, order)
+    return pl.pallas_call(
+        finish,
+        out_shape=(
+            jax.ShapeDtypeStruct((1, rank * sketch), f32),
+            jax.ShapeDtypeStruct((1, sketch, sketch), f32),
+        ),
+        in_specs=[vmem, vmem, pl.BlockSpec(memory_space=pltpu.SMEM)],
+        out_specs=(vmem, vmem),
+        name="finish",
+    )(gram, row_parts, damping)
 
 
 def solution(mesh):

time: 40.9 us -> 35.5 us (0.87)
  Pallas kernels: 36.7 us -> 34 us
  local copies, waits for them, and re-layouts: 2.65 us -> 0 us
    pallas_call x1, Pallas kernels: 36.7 us -> 30.8 us  [local(): pl.pallas_call(functools.partial(kernel, n_ex, n_mp, scaling), out_shape=...]
    pallas_call x0 -> x1, Pallas kernels: none -> 3.13 us  [local(): pl.pallas_call(finish, out_shape=(jax.ShapeDtypeStruct((1, rank * sketch)...]
    unnamed x2 -> x0, local copies, waits for them, and re-layouts: 2.65 us -> none
where the time goes in v2:
time: 35.5 us; the launch traced here: 35.2 us
  Pallas kernels  34 us (96%)
  between operations  1.29 us (4%)
    pallas_call x1, Pallas kernels, local(): pl.pallas_call(functools.partial(kernel, n_ex, n_mp, scaling), out_shape=...  30.8 us
    pallas_call x1, Pallas kernels, local(): pl.pallas_call(finish, out_shape=(jax.ShapeDtypeStruct((1, rank * sketch)...  3.13 us

profile of v2, /device:TPU:1, one launch (start us, length us, event | category | flops | bytes accessed | tf_op | source)
XLA Modules:
  0.0 35.2 jit_solution(70838954106627290)
XLA Ops:
  1.3 30.8 %trak.1 = (f32[64,64]{1,0:T(8,128)}, f32[16,1,128]{2,1,0:T(1,128)}) custom-call(bf16[1,128,4096]{2,1,0:T(8,128)(2,1)} %acts.1, bf16[1,128,1024]{2,1,0:T(8,128)(2,1)} %grads.1, bf16[1,16,4096]{2,1,0:T(8,128)(2,1)} %down.1, bf16[1,16,1024]{2,1,0:T(8,128)(2,1)} %up.1, bf16[1,64,4096]{2,1,0:T(8,128)(2,1)} %in_proj.1, bf16[1,64,1024]{2,1,0:T(8,128)(2,1)} %g_proj.1, ...), custom_call_target="tpu_custom_call" | custom-call | tf_op jit(solution)/shard_map/trak/pallas_call | solution.py:287
  32.1 3.1 %finish.1 = (f32[1,1024]{1,0:T(1,128)}, f32[1,64,64]{2,1,0:T(8,128)}) custom-call(f32[64,64]{1,0:T(8,128)} %get-tuple-element.4.gram, f32[16,1,128]{2,1,0:T(1,128)} %get-tuple-element.5.rowrecv, f32[1]{0:T(128)S(6)} %copy.10.damping), custom_call_target="tpu_custom_call" | custom-call | tf_op jit(solution)/shard_map/finish/pallas_call | solution.py:313

commit v3 on v2

--- a/solution.py
+++ b/solution.py
@@ -287,8 +287,8 @@
     gram, row_parts = pl.pallas_call(
         functools.partial(kernel, n_ex, n_mp, scaling),
         out_shape=(
-            jax.ShapeDtypeStruct((sketch, sketch), f32),
-            jax.ShapeDtypeStruct((n_mp, 1, 2 * sketch), f32),
+            pltpu.VMEM((sketch, sketch), f32),
+            pltpu.VMEM((n_mp, 1, 2 * sketch), f32),
         ),
         in_specs=[pl.BlockSpec(memory_space=pl.ANY)] * 7,
         out_specs=(vmem, vmem),
@@ -310,6 +310,8 @@
         compiler_params=pltpu.CompilerParams(collective_id=0, has_side_effects=True),
         name="trak",
     )(acts, grads, down, up, in_proj, g_proj, order)
+    gram = pltpu.with_memory_space_constraint(gram, pltpu.VMEM)
+    row_parts = pltpu.with_memory_space_constraint(row_parts, pltpu.VMEM)
     return pl.pallas_call(
         finish,
         out_shape=(

time: 35.5 us -> 34 us (0.958)
  Pallas kernels: 34 us -> 32.6 us
    pallas_call x1, Pallas kernels: 3.13 us -> 2.37 us  [local(): pl.pallas_call(finish, out_shape=(jax.ShapeDtypeStruct((1, rank * sketch)...]
    pallas_call x1, Pallas kernels: 30.8 us -> 30.2 us  [local(): pl.pallas_call(functools.partial(kernel, n_ex, n_mp, scaling), out_shape=...]
where the time goes in v3:
time: 34 us; the launch traced here: 33.9 us
  Pallas kernels  32.6 us (96%)
  between operations  1.29 us (4%)
    pallas_call x1, Pallas kernels, local(): pl.pallas_call(functools.partial(kernel, n_ex, n_mp, scaling), out_shape=...  30.2 us
    pallas_call x1, Pallas kernels, local(): pl.pallas_call(finish, out_shape=(jax.ShapeDtypeStruct((1, rank * sketch)...  2.37 us

profile of v3, /device:TPU:1, one launch (start us, length us, event | category | flops | bytes accessed | tf_op | source)
XLA Modules:
  0.0 33.9 jit_solution(1012239750571383279)
XLA Ops:
  1.3 30.2 %trak.1 = (f32[64,64]{1,0:T(8,128)S(1)}, f32[16,1,128]{2,1,0:T(1,128)S(1)}) custom-call(bf16[1,128,4096]{2,1,0:T(8,128)(2,1)} %acts.1, bf16[1,128,1024]{2,1,0:T(8,128)(2,1)} %grads.1, bf16[1,16,4096]{2,1,0:T(8,128)(2,1)} %down.1, bf16[1,16,1024]{2,1,0:T(8,128)(2,1)} %up.1, bf16[1,64,4096]{2,1,0:T(8,128)(2,1)} %in_proj.1, bf16[1,64,1024]{2,1,0:T(8,128)(2,1)} %g_proj.1, ...), custom_call_target="tpu_custom_call" | custom-call | tf_op jit(solution)/shard_map/trak/pallas_call | solution.py:287
  31.5 2.4 %finish.1 = (f32[1,1024]{1,0:T(1,128)}, f32[1,64,64]{2,1,0:T(8,128)}) custom-call(f32[64,64]{1,0:T(8,128)S(1)} %get-tuple-element.4.gram, f32[16,1,128]{2,1,0:T(1,128)S(1)} %get-tuple-element.5.rowrecv, f32[1]{0:T(128)S(6)} %copy.10.damping), custom_call_target="tpu_custom_call" | custom-call | tf_op jit(solution)/shard_map/finish/pallas_call | solution.py:315

commit v4 on v3

--- a/solution.py
+++ b/solution.py
@@ -70,13 +70,9 @@
                 blocks[b] = blocks[b] - cols[b][j] * scaled[j]
 
 
-def finish(gram, rowrecv, damping, out_f, out_r):
-    size = gram.shape[0]
-    diag = lax.broadcasted_iota(jnp.int32, (size, size), 0) == lax.broadcasted_iota(
-        jnp.int32, (size, size), 1
-    )
-    full = gram[...] + jnp.where(diag, damping[0], 0.0)
-    factor([full[b * 8 : b * 8 + 8] for b in range(size // 8)], out_r, size)
+def finish(upper, rowrecv, out_f, out_r):
+    size = upper.shape[1]
+    out_r[...] = upper[...]
     low_lane = lax.broadcasted_iota(jnp.int32, (1, 2 * size), 1) < size
     for p in range(rowrecv.shape[0] // 2):
         out_f[:, p * 2 * size : (p + 1) * 2 * size] = jnp.where(
@@ -95,7 +91,8 @@
     in_proj,
     g_proj,
     order,
-    out_s,
+    damping,
+    upper,
     rowrecv,
     a_v,
     g_v,
@@ -241,11 +238,11 @@
 
     lane = lax.broadcasted_iota(jnp.int32, (8, 2 * sketch), 1)
     turned = jnp.concatenate([mine[:, sketch:], mine[:, :sketch]], axis=1)
-    lower = jnp.where(lane < sketch, mine, turned)
-    upper = jnp.where(lane < sketch, turned, mine)
+    first = jnp.where(lane < sketch, mine, turned)
+    second = jnp.where(lane < sketch, turned, mine)
     for r in range(8):
-        rowsend[r] = lower[r : r + 1]
-        rowsend[r + 8] = upper[r : r + 1]
+        rowsend[r] = first[r : r + 1]
+        rowsend[r + 8] = second[r : r + 1]
 
     def send_rows(s, _):
         dst = lax.rem(mp + outward(s, n_mp), n_mp)
@@ -271,7 +268,12 @@
         preferred_element_type=jnp.float32,
         precision=lax.Precision.HIGHEST,
     )
-    out_s[...] = (square[:sketch, :sketch] + square[sketch:, sketch:]) * (1.0 / (n_ex * 16))
+    gram = (square[:sketch, :sketch] + square[sketch:, sketch:]) * (1.0 / (n_ex * 16))
+    diag = lax.broadcasted_iota(jnp.int32, (sketch, sketch), 0) == lax.broadcasted_iota(
+        jnp.int32, (sketch, sketch), 1
+    )
+    system = gram + jnp.where(diag, damping[0], 0.0)
+    factor([system[b * 8 : b * 8 + 8] for b in range(sketch // 8)], upper, sketch)
     wait_bytes(rowrecv, n_mp - 1, recv_sem.at[2])
     wait_bytes(zsend, n_mp - 1, send_sem.at[0])
     wait_bytes(xbuf, n_ex - 1, send_sem.at[1])
@@ -284,13 +286,13 @@
     scaling = 1.0 / math.sqrt(2.0 * EXAMPLE_LENGTH * n_mp)
     f32 = jnp.float32
     vmem = pl.BlockSpec(memory_space=pltpu.VMEM)
-    gram, row_parts = pl.pallas_call(
+    triangle, row_parts = pl.pallas_call(
         functools.partial(kernel, n_ex, n_mp, scaling),
         out_shape=(
-            pltpu.VMEM((sketch, sketch), f32),
+            pltpu.VMEM((1, sketch, sketch), f32),
             pltpu.VMEM((n_mp, 1, 2 * sketch), f32),
         ),
-        in_specs=[pl.BlockSpec(memory_space=pl.ANY)] * 7,
+        in_specs=[pl.BlockSpec(memory_space=pl.ANY)] * 7 + [pl.BlockSpec(memory_space=pltpu.SMEM)],
         out_specs=(vmem, vmem),
         scratch_shapes=[
             pltpu.VMEM(acts.shape[1:], acts.dtype),
@@ -309,8 +311,8 @@
         ],
         compiler_params=pltpu.CompilerParams(collective_id=0, has_side_effects=True),
         name="trak",
-    )(acts, grads, down, up, in_proj, g_proj, order)
-    gram = pltpu.with_memory_space_constraint(gram, pltpu.VMEM)
+    )(acts, grads, down, up, in_proj, g_proj, order, damping)
+    triangle = pltpu.with_memory_space_constraint(triangle, pltpu.VMEM)
     row_parts = pltpu.with_memory_space_constraint(row_parts, pltpu.VMEM)
     return pl.pallas_call(
         finish,
@@ -318,10 +320,10 @@
             jax.ShapeDtypeStruct((1, rank * sketch), f32),
             jax.ShapeDtypeStruct((1, sketch, sketch), f32),
         ),
-        in_specs=[vmem, vmem, pl.BlockSpec(memory_space=pltpu.SMEM)],
+        in_specs=[vmem, vmem],
         out_specs=(vmem, vmem),
         name="finish",
-    )(gram, row_parts, damping)
+    )(triangle, row_parts)
 
 
 def solution(mesh):

time: 34 us -> 34 us (level)
    pallas_call x1, Pallas kernels: 30.2 us -> 32 us  [local(): pl.pallas_call(functools.partial(kernel, n_ex, n_mp, scaling), out_shape=...]
    pallas_call x1, Pallas kernels: 2.37 us -> 0.62 us  [local(): pl.pallas_call(finish, out_shape=(jax.ShapeDtypeStruct((1, rank * sketch)...]
where the time goes in v4:
time: 34 us; the launch traced here: 33.9 us
  Pallas kernels  32.6 us (96%)
  between operations  1.29 us (4%)
    pallas_call x1, Pallas kernels, local(): pl.pallas_call(functools.partial(kernel, n_ex, n_mp, scaling), out_shape=...  32 us

profile of v4, /device:TPU:1, one launch (start us, length us, event | category | flops | bytes accessed | tf_op | source)
XLA Modules:
  0.0 33.9 jit_solution(9777111871398692438)
XLA Ops:
  1.3 32.0 %trak.1 = (f32[1,64,64]{2,1,0:T(8,128)S(1)}, f32[16,1,128]{2,1,0:T(1,128)S(1)}) custom-call(bf16[1,128,4096]{2,1,0:T(8,128)(2,1)} %acts.1, bf16[1,128,1024]{2,1,0:T(8,128)(2,1)} %grads.1, bf16[1,16,4096]{2,1,0:T(8,128)(2,1)} %down.1, bf16[1,16,1024]{2,1,0:T(8,128)(2,1)} %up.1, bf16[1,64,4096]{2,1,0:T(8,128)(2,1)} %in_proj.1, bf16[1,64,1024]{2,1,0:T(8,128)(2,1)} %g_proj.1, ...), custom_call_target="tpu_custom_call" | custom-call | tf_op jit(solution)/shard_map/trak/pallas_call | solution.py:289
  33.2 0.6 %finish.1 = (f32[1,1024]{1,0:T(1,128)}, f32[1,64,64]{2,1,0:T(8,128)}) custom-call(f32[1,64,64]{2,1,0:T(8,128)S(1)} %get-tuple-element.4.upper, f32[16,1,128]{2,1,0:T(1,128)S(1)} %get-tuple-element.5.rowrecv), custom_call_target="tpu_custom_call" | custom-call | tf_op jit(solution)/shard_map/finish/pallas_call | solution.py:317

commit v5 on v4

--- a/solution.py
+++ b/solution.py
@@ -100,6 +100,8 @@
     wg_v,
     zsend,
     zrecv,
+    relaysend,
+    relayrecv,
     fbuf,
     xbuf,
     rowsend,
@@ -145,7 +147,9 @@
 
         lax.fori_loop(0, n - 1, body, 0)
 
-    greet("mp", n_mp, mp)
+    for far in range(n_mp // 4, 0, -1):
+        for dst in (lax.rem(mp + far, n_mp), lax.rem(mp + n_mp - far, n_mp)):
+            pl.semaphore_signal(barrier, inc=1, device_id={"mp": dst}, device_id_type=MESH)
     order_copy.start()
     for copy in g_copies:
         copy.start()
@@ -199,26 +203,39 @@
     right_h, right_l = halves(right)
     part = nt(left_h, right_h) + (nt(left_h, right_l) + nt(left_l, right_h))
     tiles = jnp.concatenate([part[: rank * 8], part[rank * 8 :]], axis=1)
-    zsend[...] = tiles.reshape(rank, 8, 2 * sketch)
-
-    pl.semaphore_wait(barrier, n_mp + n_ex - 2)
-
-    def send_z(s, _):
-        dst = lax.rem(mp + outward(s, n_mp), n_mp)
+    half = n_mp // 2
+    for c in range(rank):
+        zsend[c % half, c // half] = tiles[c * 8 : c * 8 + 8]
+
+    reach = half // 2
+    pl.semaphore_wait(barrier, 2 * reach + n_ex - 1)
+
+    offsets = [a for far in range(reach, 0, -1) for a in (far, -far) if a != -reach]
+    for k, a in enumerate(offsets):
+        relay = lax.rem(mp + n_mp - a, n_mp)
         pltpu.make_async_remote_copy(
-            src_ref=zsend.at[dst],
-            dst_ref=zrecv.at[mp],
+            src_ref=zsend.at[lax.rem(relay + reach, half)],
+            dst_ref=zrecv.at[k],
             send_sem=send_sem.at[0],
             recv_sem=recv_sem.at[0],
-            device_id={"mp": dst},
+            device_id={"mp": relay},
             device_id_type=MESH,
         ).start()
-        return 0
-
-    lax.fori_loop(0, n_mp - 1, send_z, 0)
-    zrecv[mp] = zsend[mp]
-    wait_bytes(zrecv, n_mp - 1, recv_sem.at[0])
-    mine = jnp.sum(zrecv[...], axis=0)
+    group = lax.rem(mp + reach, half)
+    total = zsend[group]
+    wait_bytes(zrecv, len(offsets), recv_sem.at[0])
+    relaysend[...] = total + jnp.sum(zrecv[...], axis=0)
+    for q in range(2):
+        pltpu.make_async_remote_copy(
+            src_ref=relaysend.at[q],
+            dst_ref=relayrecv.at[mp // half],
+            send_sem=send_sem.at[3],
+            recv_sem=recv_sem.at[3],
+            device_id={"mp": group + q * half},
+            device_id_type=MESH,
+        ).start()
+    wait_bytes(relayrecv, 2, recv_sem.at[3])
+    mine = relayrecv[0] + relayrecv[1]
     fbuf[...] = mine
     xbuf[ex] = mine
 
@@ -275,7 +292,8 @@
     system = gram + jnp.where(diag, damping[0], 0.0)
     factor([system[b * 8 : b * 8 + 8] for b in range(sketch // 8)], upper, sketch)
     wait_bytes(rowrecv, n_mp - 1, recv_sem.at[2])
-    wait_bytes(zsend, n_mp - 1, send_sem.at[0])
+    wait_bytes(zrecv, n_mp // 2 - 1, send_sem.at[0])
+    wait_bytes(relaysend, 2, send_sem.at[3])
     wait_bytes(xbuf, n_ex - 1, send_sem.at[1])
     wait_bytes(rowsend, n_mp - 1, send_sem.at[2])
 
@@ -299,15 +317,17 @@
             pltpu.VMEM(grads.shape[1:], grads.dtype),
             pltpu.VMEM((rank + sketch, acts.shape[2]), acts.dtype),
             pltpu.VMEM((rank + sketch, grads.shape[2]), grads.dtype),
-            pltpu.VMEM((n_mp, 8, 2 * sketch), f32),
-            pltpu.VMEM((n_mp, 8, 2 * sketch), f32),
+            pltpu.VMEM((n_mp // 2, 2, 8, 2 * sketch), f32),
+            pltpu.VMEM((n_mp // 2 - 1, 2, 8, 2 * sketch), f32),
+            pltpu.VMEM((2, 8, 2 * sketch), f32),
+            pltpu.VMEM((2, 8, 2 * sketch), f32),
             pltpu.VMEM((8, 2 * sketch), f32),
             pltpu.VMEM((n_ex, 8, 2 * sketch), f32),
             pltpu.VMEM((n_mp, 1, 2 * sketch), f32),
             pltpu.VMEM(order.shape, order.dtype),
             pltpu.SemaphoreType.DMA((4 + 3 * CHUNKS,)),
-            pltpu.SemaphoreType.DMA((3,)),
-            pltpu.SemaphoreType.DMA((3,)),
+            pltpu.SemaphoreType.DMA((4,)),
+            pltpu.SemaphoreType.DMA((4,)),
         ],
         compiler_params=pltpu.CompilerParams(collective_id=0, has_side_effects=True),
         name="trak",

time: 34 us -> 34 us (level)
  no operation moved by 1% of the time
where the time goes in v5:
time: 34 us; the launch traced here: 33.9 us
  Pallas kernels  32.6 us (96%)
  between operations  1.29 us (4%)
    pallas_call x1, Pallas kernels, local(): pl.pallas_call(functools.partial(kernel, n_ex, n_mp, scaling), out_shape=...  31.9 us

profile of v5, /device:TPU:1, one launch (start us, length us, event | category | flops | bytes accessed | tf_op | source)
XLA Modules:
  0.0 33.9 jit_solution(11497699360396304829)
XLA Ops:
  1.3 31.9 %trak.1 = (f32[1,64,64]{2,1,0:T(8,128)S(1)}, f32[16,1,128]{2,1,0:T(1,128)S(1)}) custom-call(bf16[1,128,4096]{2,1,0:T(8,128)(2,1)} %acts.1, bf16[1,128,1024]{2,1,0:T(8,128)(2,1)} %grads.1, bf16[1,16,4096]{2,1,0:T(8,128)(2,1)} %down.1, bf16[1,16,1024]{2,1,0:T(8,128)(2,1)} %up.1, bf16[1,64,4096]{2,1,0:T(8,128)(2,1)} %in_proj.1, bf16[1,64,1024]{2,1,0:T(8,128)(2,1)} %g_proj.1, ...), custom_call_target="tpu_custom_call" | custom-call | tf_op jit(solution)/shard_map/trak/pallas_call | solution.py:307
  33.2 0.6 %finish.1 = (f32[1,1024]{1,0:T(1,128)}, f32[1,64,64]{2,1,0:T(8,128)}) custom-call(f32[1,64,64]{2,1,0:T(8,128)S(1)} %get-tuple-element.4.upper, f32[16,1,128]{2,1,0:T(1,128)S(1)} %get-tuple-element.5.rowrecv), custom_call_target="tpu_custom_call" | custom-call | tf_op jit(solution)/shard_map/finish/pallas_call | solution.py:337

commit v6 on v5

--- a/solution.py
+++ b/solution.py
@@ -23,7 +23,7 @@
 
 
 def outward(step, n):
-    turn = lax.rem(step + 1, 2)
+    turn = (step + 1) % 2
     return n // 2 + ((step + 1) // 2) * (1 - 2 * turn)
 
 
@@ -251,7 +251,8 @@
         ).start()
         return 0
 
-    lax.fori_loop(0, n_ex - 1, send_x, 0)
+    for s in range(n_ex - 1):
+        send_x(s, 0)
 
     lane = lax.broadcasted_iota(jnp.int32, (8, 2 * sketch), 1)
     turned = jnp.concatenate([mine[:, sketch:], mine[:, :sketch]], axis=1)

time: 34 us -> 34 us (level)
  no operation moved by 1% of the time
where the time goes in v6:
time: 34 us; the launch traced here: 33.9 us
  Pallas kernels  32.6 us (96%)
  between operations  1.29 us (4%)
    pallas_call x1, Pallas kernels, local(): pl.pallas_call(functools.partial(kernel, n_ex, n_mp, scaling), out_shape=...  31.9 us

profile of v6, /device:TPU:1, one launch (start us, length us, event | category | flops | bytes accessed | tf_op | source)
XLA Modules:
  0.0 33.9 jit_solution(2916101153174635055)
XLA Ops:
  1.3 31.9 %trak.1 = (f32[1,64,64]{2,1,0:T(8,128)S(1)}, f32[16,1,128]{2,1,0:T(1,128)S(1)}) custom-call(bf16[1,128,4096]{2,1,0:T(8,128)(2,1)} %acts.1, bf16[1,128,1024]{2,1,0:T(8,128)(2,1)} %grads.1, bf16[1,16,4096]{2,1,0:T(8,128)(2,1)} %down.1, bf16[1,16,1024]{2,1,0:T(8,128)(2,1)} %up.1, bf16[1,64,4096]{2,1,0:T(8,128)(2,1)} %in_proj.1, bf16[1,64,1024]{2,1,0:T(8,128)(2,1)} %g_proj.1, ...), custom_call_target="tpu_custom_call" | custom-call | tf_op jit(solution)/shard_map/trak/pallas_call | solution.py:308
  33.2 0.6 %finish.1 = (f32[1,1024]{1,0:T(1,128)}, f32[1,64,64]{2,1,0:T(8,128)}) custom-call(f32[1,64,64]{2,1,0:T(8,128)S(1)} %get-tuple-element.4.upper, f32[16,1,128]{2,1,0:T(1,128)S(1)} %get-tuple-element.5.rowrecv), custom_call_target="tpu_custom_call" | custom-call | tf_op jit(solution)/shard_map/finish/pallas_call | solution.py:338
